TPU v7x, 32 devices: a whole 2x2x4 slice. The times are simulated.
32 devices in a mesh: seq: 2 (over y), ctx: 4 (over z), tp: 4 (over x, core).
Axes of the slice: x: 2, y: 2, z: 4, core: 2. Of those that a mesh axis runs over, the one named last changes fastest.
Arguments:
- tokens: bfloat16 [2048, 2048], P(('seq', 'ctx')), may hold values from -6 to 6
- query_weight: bfloat16 [2048, 2048], P(('seq', 'ctx'), 'tp'), may hold values from -0.125 to 0.125
- key_weight: bfloat16 [2048, 2048], P(('seq', 'ctx'), 'tp'), may hold values from -0.125 to 0.125
- value_weight: bfloat16 [2048, 2048], P(('seq', 'ctx'), 'tp'), may hold values from -0.125 to 0.125
- output_weight: bfloat16 [2048, 2048], P('tp', ('seq', 'ctx')), may hold values from -1.5 to 1.5
- gate_weight: bfloat16 [2048, 8192], P(('seq', 'ctx'), 'tp'), may hold values from -0.125 to 0.125
- up_weight: bfloat16 [2048, 8192], P(('seq', 'ctx'), 'tp'), may hold values from -0.125 to 0.125
- down_weight: bfloat16 [8192, 2048], P('tp', ('seq', 'ctx')), may hold values from -0.0625 to 0.0625
- attention_gain: bfloat16 [2048], P(('seq', 'ctx')), may hold values from 0.25 to 1.75
- feedforward_gain: bfloat16 [2048], P(('seq', 'ctx')), may hold values from 0.25 to 1.75
- order: int32 [8], replicated, may hold values from 0 to 7, each once
- cotangent: bfloat16 [2048, 2048], P(('seq', 'ctx')), may hold values from -6 to 6
Outputs:
- block_output: bfloat16 [2048, 2048], P(('seq', 'ctx'))
- input_grad: float32 [2048, 2048], P(('seq', 'ctx'))
- query_weight_grad: float32 [2048, 2048], P(('seq', 'ctx'), 'tp')
- key_weight_grad: float32 [2048, 2048], P(('seq', 'ctx'), 'tp')
- value_weight_grad: float32 [2048, 2048], P(('seq', 'ctx'), 'tp')
- output_weight_grad: float32 [2048, 2048], P('tp', ('seq', 'ctx'))
- gate_weight_grad: float32 [2048, 8192], P(('seq', 'ctx'), 'tp')
- up_weight_grad: float32 [2048, 8192], P(('seq', 'ctx'), 'tp')
- down_weight_grad: float32 [8192, 2048], P('tp', ('seq', 'ctx'))
- attention_gain_grad: float32 [2048], P(('seq', 'ctx'))
- feedforward_gain_grad: float32 [2048], P(('seq', 'ctx'))
Inputs may be any that keep to these rules, and one draw needn't show every extreme that they name: order holds every block position of a sequence once; the device of ctx index c stores blocks 2c and 2c + 1 of each sequence.
All inputs are finite; a program needn't handle non-finite values.
Results may differ from a plain program's by a relative error of at most 0.02.
Values may be sent and summed in bfloat16 or wider, within the bound.
No kernel may reach another device: no remote copies, remote signals or barrier semaphores. Data moves between devices by JAX's collectives and lax.ppermute only.
A program may use at most 128 MiB of HBM per device.

v0:
```python
from functools import partial
import jax
import jax.numpy as jnp
from jax import lax
from jax.sharding import PartitionSpec as P

HD = 64
BLOCK = 128
THETA = 130000.0
EPS = 1e-05


def shifted(block, axis, distance):
    devices = range(lax.axis_size(axis))
    route = [((i - distance) % len(devices), i) for i in devices]
    return lax.ppermute(block, axis, route)


def rms_norm(hidden, gain):
    return hidden * lax.rsqrt(jnp.mean(hidden * hidden, axis=-1, keepdims=True) + EPS) * gain


def rotary(values, places):
    row_count = values.shape[0]
    by_heads = values.reshape(row_count, -1, HD)
    halfway = HD // 2
    inverse = THETA ** (-(jnp.arange(halfway, dtype=jnp.float32) * 2.0) / HD)
    angle = places.astype(jnp.float32)[:, None] * inverse[None, :]
    angle = jnp.concatenate([angle, angle], axis=1)
    cosine = jnp.cos(angle)[:, None, :]
    sine = jnp.sin(angle)[:, None, :]
    turned = jnp.concatenate([-by_heads[..., halfway:], by_heads[..., :halfway]], axis=-1)
    return (by_heads * cosine + turned * sine).reshape(row_count, -1)


def gated(gate, upward):
    return jax.nn.silu(gate) * upward


def product(left, right):
    return jnp.dot(left, right, preferred_element_type=jnp.float32)


def contract_rows(left, right):
    return lax.dot_general(
        left, right, (((0,), (0,)), ((), ())), preferred_element_type=jnp.float32
    )


def contract_cols(left, right):
    return lax.dot_general(
        left, right, (((1,), (1,)), ((), ())), preferred_element_type=jnp.float32
    )


def key_places(order, first_row, row_total):
    stored = first_row + jnp.arange(row_total, dtype=jnp.int32)
    group_slot = stored // BLOCK
    slot_table = jnp.arange(order.shape[0], dtype=jnp.int32)
    block_place = jnp.sum(
        jnp.where(group_slot[:, None] == slot_table[None, :], order[None, :], 0), axis=1
    )
    return block_place * BLOCK + stored % BLOCK


def exp_scores(query_heads, query_places, key_rows, key_pos):
    row_total = key_rows.shape[0]
    key_heads = key_rows.reshape(row_total, -1, HD)
    scores = (
        jnp.einsum("qhd,khd->hqk", query_heads, key_heads, preferred_element_type=jnp.float32)
        * 0.125
    )
    allowed = query_places[:, None] >= key_pos[None, :]
    return (jnp.where(allowed[None], jnp.exp(scores), 0.0), key_heads)


def per_device(
    tokens,
    query_weight,
    key_weight,
    value_weight,
    output_weight,
    gate_weight,
    up_weight,
    down_weight,
    attention_gain,
    feedforward_gain,
    order,
    cotangent,
):
    rows_local = tokens.shape[0]
    ctx_index = lax.axis_index("ctx")
    ctx_total = lax.axis_size("ctx")
    gathered = (
        lax.all_gather(query_weight, ("seq", "ctx"), axis=0, tiled=True),
        lax.all_gather(key_weight, ("seq", "ctx"), axis=0, tiled=True),
        lax.all_gather(value_weight, ("seq", "ctx"), axis=0, tiled=True),
        lax.all_gather(output_weight, ("seq", "ctx"), axis=1, tiled=True),
        lax.all_gather(gate_weight, ("seq", "ctx"), axis=0, tiled=True),
        lax.all_gather(up_weight, ("seq", "ctx"), axis=0, tiled=True),
        lax.all_gather(down_weight, ("seq", "ctx"), axis=1, tiled=True),
        lax.all_gather(attention_gain, ("seq", "ctx"), axis=0, tiled=True),
        lax.all_gather(feedforward_gain, ("seq", "ctx"), axis=0, tiled=True),
    )
    (
        full_query,
        full_key,
        full_value,
        full_output,
        full_gate,
        full_up,
        full_down,
        gain_first,
        gain_second,
    ) = gathered
    inputs = tokens.astype(jnp.float32)
    query_places = key_places(order, ctx_index * rows_local, rows_local)
    normed_value, norm_back_first = jax.vjp(rms_norm, inputs, gain_first.astype(jnp.float32))
    normed = normed_value.astype(jnp.bfloat16)
    rope_here = partial(rotary, places=query_places)
    query_rot, query_back = jax.vjp(rope_here, product(normed, full_query))
    key_rot, key_back = jax.vjp(rope_here, product(normed, full_key))
    value_rows = product(normed, full_value).astype(jnp.bfloat16)
    query_rows = query_rot.astype(jnp.bfloat16)
    key_rows = key_rot.astype(jnp.bfloat16)
    width = query_rows.shape[1]
    head_count = width // HD
    query_heads = query_rows.reshape(rows_local, head_count, HD)
    packed = jnp.stack([key_rows, value_rows])
    empty_totals = jnp.zeros((rows_local, head_count), jnp.float32)
    empty_numerator = jnp.zeros((rows_local, width), jnp.float32)
    arrived = lax.all_gather(packed, "ctx", axis=1, tiled=True)
    row_total = arrived.shape[1]

    def one_block(block_index, partial_state):
        first_row = block_index * rows_local
        section = lax.dynamic_slice_in_dim(arrived, first_row, rows_local, 1)
        key_pos = key_places(order, first_row, rows_local)
        weights, key_heads = exp_scores(query_heads, query_places, section[0], key_pos)
        value_heads = section[1].reshape(rows_local, -1, HD)
        totals, numerator = partial_state
        totals = totals + jnp.sum(weights, axis=2).T
        numerator = numerator + jnp.einsum(
            "hqk,khd->qhd",
            weights.astype(jnp.bfloat16),
            value_heads,
            preferred_element_type=jnp.float32,
        ).reshape(rows_local, width)
        return (totals, numerator)

    totals, numerator = lax.fori_loop(
        0, row_total // rows_local, one_block, (empty_totals, empty_numerator)
    )
    numerator_heads = numerator.reshape(rows_local, head_count, HD)
    mixed = (numerator_heads / totals[:, :, None]).astype(jnp.bfloat16).reshape(rows_local, width)
    middle = inputs + lax.psum(product(mixed, full_output), "tp")
    normed_two_value, norm_back_second = jax.vjp(rms_norm, middle, gain_second.astype(jnp.float32))
    normed_two = normed_two_value.astype(jnp.bfloat16)
    activated, gated_back = jax.vjp(
        gated, product(normed_two, full_gate), product(normed_two, full_up)
    )
    hidden = activated.astype(jnp.bfloat16)
    block_output = middle + lax.psum(product(hidden, full_down).astype(jnp.bfloat16), "tp").astype(
        jnp.float32
    )
    back_weights = (
        lax.all_gather(query_weight, ("seq", "ctx"), axis=0, tiled=True),
        lax.all_gather(key_weight, ("seq", "ctx"), axis=0, tiled=True),
        lax.all_gather(value_weight, ("seq", "ctx"), axis=0, tiled=True),
        lax.all_gather(output_weight, ("seq", "ctx"), axis=1, tiled=True),
        lax.all_gather(gate_weight, ("seq", "ctx"), axis=0, tiled=True),
        lax.all_gather(up_weight, ("seq", "ctx"), axis=0, tiled=True),
        lax.all_gather(down_weight, ("seq", "ctx"), axis=1, tiled=True),
        lax.all_gather(attention_gain, ("seq", "ctx"), axis=0, tiled=True),
        lax.all_gather(feedforward_gain, ("seq", "ctx"), axis=0, tiled=True),
    )
    (
        back_query,
        back_key,
        back_value,
        back_output,
        back_gate,
        back_up,
        back_down,
        gain_unused,
        gain_spare,
    ) = back_weights
    down_grad = contract_rows(hidden, cotangent)
    hidden_grad = contract_cols(cotangent, back_down)
    gate_grad, upward_grad = gated_back(hidden_grad)
    gate_grad = gate_grad.astype(jnp.bfloat16)
    upward_grad = upward_grad.astype(jnp.bfloat16)
    gate_wgrad = contract_rows(normed_two, gate_grad)
    upward_wgrad = contract_rows(normed_two, upward_grad)
    normed_two_grad = lax.psum(
        contract_cols(gate_grad, back_gate) + contract_cols(upward_grad, back_up), "tp"
    )
    middle_norm_grad, second_gain_grad = norm_back_second(normed_two_grad)
    middle_grad = cotangent.astype(jnp.float32) + middle_norm_grad
    branch_grad = middle_grad.astype(jnp.bfloat16)
    output_wgrad = contract_rows(mixed, branch_grad)
    mixed_grad = contract_cols(branch_grad, back_output).reshape(rows_local, head_count, HD)
    numerator_grad = (mixed_grad / totals[:, :, None]).astype(jnp.bfloat16)
    totals_grad = -jnp.sum(mixed_grad * numerator_heads, axis=2) / (totals * totals)
    totals_grad_heads = totals_grad.T[:, :, None]

    def visit(turn_index, state):
        visiting, carried, query_acc = state
        source = (ctx_index - turn_index) % ctx_total
        key_pos = key_places(order, source * rows_local, rows_local)
        weights, key_heads = exp_scores(query_heads, query_places, visiting[0], key_pos)
        value_heads = visiting[1].reshape(rows_local, -1, HD)
        through = jnp.einsum(
            "qhd,khd->hqk", numerator_grad, value_heads, preferred_element_type=jnp.float32
        )
        slopes = (weights * (through + totals_grad_heads)).astype(jnp.bfloat16)
        query_acc = (
            query_acc
            + jnp.einsum("hqk,khd->qhd", slopes, key_heads, preferred_element_type=jnp.float32)
            * 0.125
        )
        key_term = (
            jnp.einsum("hqk,qhd->khd", slopes, query_heads, preferred_element_type=jnp.float32)
            * 0.125
        )
        value_term = jnp.einsum(
            "hqk,qhd->khd",
            weights.astype(jnp.bfloat16),
            numerator_grad,
            preferred_element_type=jnp.float32,
        )
        carried = carried + jnp.stack(
            [key_term.reshape(rows_local, width), value_term.reshape(rows_local, width)]
        )
        visiting = shifted(visiting, "ctx", 1)
        carried = shifted(carried, "ctx", 1)
        return (visiting, carried, query_acc)

    start_state = (
        packed,
        jnp.zeros((2, rows_local, width), jnp.float32),
        jnp.zeros((rows_local, head_count, HD), jnp.float32),
    )
    ended, key_value_grad, query_acc = lax.fori_loop(0, ctx_total, visit, start_state)
    query_proj_grad = query_back(query_acc.reshape(rows_local, width))[0].astype(jnp.bfloat16)
    key_proj_grad = key_back(key_value_grad[0])[0].astype(jnp.bfloat16)
    value_grad = key_value_grad[1].astype(jnp.bfloat16)
    query_wgrad = contract_rows(normed, query_proj_grad)
    key_wgrad = contract_rows(normed, key_proj_grad)
    value_wgrad = contract_rows(normed, value_grad)
    normed_grad = lax.psum(
        (
            contract_cols(query_proj_grad, back_query)
            + contract_cols(key_proj_grad, back_key)
            + contract_cols(value_grad, back_value)
        ).astype(jnp.bfloat16),
        "tp",
    ).astype(jnp.float32)
    input_norm_grad, first_gain_grad = norm_back_first(normed_grad)
    input_grad = middle_grad + input_norm_grad
    scattered = (
        lax.psum_scatter(
            query_wgrad.astype(jnp.bfloat16), ("seq", "ctx"), scatter_dimension=0, tiled=True
        ).astype(jnp.float32),
        lax.psum_scatter(
            key_wgrad.astype(jnp.bfloat16), ("seq", "ctx"), scatter_dimension=0, tiled=True
        ).astype(jnp.float32),
        lax.psum_scatter(
            value_wgrad.astype(jnp.bfloat16), ("seq", "ctx"), scatter_dimension=0, tiled=True
        ).astype(jnp.float32),
        lax.psum_scatter(
            output_wgrad.astype(jnp.bfloat16), ("seq", "ctx"), scatter_dimension=1, tiled=True
        ).astype(jnp.float32),
        lax.psum_scatter(
            gate_wgrad.astype(jnp.bfloat16), ("seq", "ctx"), scatter_dimension=0, tiled=True
        ).astype(jnp.float32),
        lax.psum_scatter(
            upward_wgrad.astype(jnp.bfloat16), ("seq", "ctx"), scatter_dimension=0, tiled=True
        ).astype(jnp.float32),
        lax.psum_scatter(
            down_grad.astype(jnp.bfloat16), ("seq", "ctx"), scatter_dimension=1, tiled=True
        ).astype(jnp.float32),
        lax.psum_scatter(
            first_gain_grad.astype(jnp.bfloat16), ("seq", "ctx"), scatter_dimension=0, tiled=True
        ).astype(jnp.float32),
        lax.psum_scatter(
            second_gain_grad.astype(jnp.bfloat16), ("seq", "ctx"), scatter_dimension=0, tiled=True
        ).astype(jnp.float32),
    )
    return (
        block_output.astype(jnp.bfloat16),
        input_grad,
        scattered[0],
        scattered[1],
        scattered[2],
        scattered[3],
        scattered[4],
        scattered[5],
        scattered[6],
        scattered[7],
        scattered[8],
    )


def solution(mesh):
    placed = (
        P(("seq", "ctx"), None),
        P(("seq", "ctx"), "tp"),
        P(("seq", "ctx"), "tp"),
        P(("seq", "ctx"), "tp"),
        P("tp", ("seq", "ctx")),
        P(("seq", "ctx"), "tp"),
        P(("seq", "ctx"), "tp"),
        P("tp", ("seq", "ctx")),
        P(("seq", "ctx")),
        P(("seq", "ctx")),
        P(),
        P(("seq", "ctx"), None),
    )
    return jax.shard_map(
        per_device,
        mesh=mesh,
        in_specs=placed,
        out_specs=(
            P(("seq", "ctx"), None),
            P(("seq", "ctx"), None),
            P(("seq", "ctx"), "tp"),
            P(("seq", "ctx"), "tp"),
            P(("seq", "ctx"), "tp"),
            P("tp", ("seq", "ctx")),
            P(("seq", "ctx"), "tp"),
            P(("seq", "ctx"), "tp"),
            P("tp", ("seq", "ctx")),
            P(("seq", "ctx")),
            P(("seq", "ctx")),
        ),
        check_vma=False,
    )
```

profile of v0, /device:TPU:0, one launch (start us, length us, event | category | flops | bytes accessed | tf_op | source)
XLA Modules:
  0.0 1750.2 jit_solution(15163281541108414726)
XLA Ops:
  10.1 22.3 %all-gather = bf16[8,1,256]{2,1,0:T(2,128)(2,1)S(1)} all-gather(bf16[1,1,256]{2,1,0:T(2,128)(2,1)S(1)} %reshape.359), channel_id=1, replica_groups=mesh['seq'=2,'ctx'=4,'tp'=4] {'seq','ctx'}, dimensions={0}, use_global_device_ids=true | all-gather | bytes 4608 | tf_op jit(solution)/shard_map/all_gather | solution.py:102
  34.6 27.6 %all-gather.11.cloned.1.call-done = bf16[2048,512]{1,0:T(8,128)(2,1)} async-done(((bf16[256,512]{1,0:T(8,128)(2,1)}), bf16[2048,512]{1,0:T(8,128)(2,1)}) %all-gather.11.cloned.1.call-update) | async-done | bytes 2097168 | tf_op jit(solution)/shard_map/all_gather | solution.py:96
  62.2 2.3 fusion.57
  64.7 47.4 %all-gather.17.cloned.1.call-done = bf16[2048,512]{1,0:T(8,128)(2,1)} async-done(((bf16[256,512]{1,0:T(8,128)(2,1)}), bf16[2048,512]{1,0:T(8,128)(2,1)}) %all-gather.17.cloned.1.call-update) | async-done | bytes 2097168 | tf_op jit(solution)/shard_map/all_gather | solution.py:95
  112.1 2.3 fusion.54
  118.9 2.1 copy.65
  121.0 2.1 add_convert_fusion.3
  123.1 39.0 %all-gather.13.cloned.1.call-done = bf16[2048,512]{1,0:T(8,128)(2,1)} async-done(((bf16[256,512]{1,0:T(8,128)(2,1)}), bf16[2048,512]{1,0:T(8,128)(2,1)}) %all-gather.13.cloned.1.call-update) | async-done | bytes 2097168 | tf_op jit(solution)/shard_map/all_gather | solution.py:97
  162.1 2.3 fusion.36
  166.1 43.8 %all-gather.15.cloned.1.call-done = bf16[2,1024,512]{2,1,0:T(8,128)(2,1)} async-done(((bf16[2,256,512]{2,1,0:T(8,128)(2,1)}), bf16[2,1024,512]{2,1,0:T(8,128)(2,1)}) %all-gather.15.cloned.1.call-update) | async-done | bytes 2097168 | tf_op jit(solution)/shard_map/all_gather | solution.py:132
  209.9 22.9 %while.39 = (s32[]{:T(128)}, f32[256,8]{0,1:T(8,128)S(1)}, f32[256,512]{0,1:T(8,128)}, s32[256]{0:T(256)}, s32[8]{0:T(128)}, /*index=5*/bf16[2,1024,512]{2,1,0:T...) while((s32[]{:T(128)}, f32[256,8]{0,1:T(8,128)S(1)}, ...), condition=%wide.region_5.6_spmd.clone, body=%wide.region_2.5_spmd.clone.sunk | while | flops 137706752 | bytes 9411818 | solution.py:151
  218.9 1.9 bitcast_add_fusion.5
  224.9 1.9 bitcast_add_fusion.5
  230.8 1.9 bitcast_add_fusion.5
  233.8 27.7 %all-gather.19.cloned.1.call-done = bf16[512,2048]{1,0:T(8,128)(2,1)} async-done(((bf16[512,256]{1,0:T(8,128)(2,1)}), bf16[512,2048]{1,0:T(8,128)(2,1)}) %all-gather.19.cloned.1.call-update) | async-done | bytes 2097168 | tf_op jit(solution)/shard_map/all_gather | solution.py:98
  261.5 3.6 fusion.65
  267.5 18.2 %all-gather.1 = bf16[8,1,256]{2,1,0:T(2,128)(2,1)S(1)} all-gather(bf16[1,1,256]{2,1,0:T(2,128)(2,1)S(1)} %reshape.361), channel_id=1, replica_groups=mesh['seq'=2,'ctx'=4,'tp'=4] {'seq','ctx'}, dimensions={0}, use_global_device_ids=true | all-gather | bytes 4608 | tf_op jit(solution)/shard_map/all_gather | solution.py:103
  286.3 28.6 %all-reduce.12.cloned.1.call-done = f32[256,2048]{1,0:T(8,128)} async-done(((f32[256,2048]{1,0:T(8,128)}), f32[256,2048]{1,0:T(8,128)}) %all-reduce.12.cloned.1.call-update) | async-done | bytes 2097168 | tf_op jit(solution)/shard_map/psum | solution.py:156
  314.9 2.0 multiply_reduce_fusion.2
  317.8 124.5 %all-gather.21.cloned.1.call-done = bf16[2048,2048]{1,0:T(8,128)(2,1)} async-done(((bf16[256,2048]{1,0:T(8,128)(2,1)}), bf16[2048,2048]{1,0:T(8,128)(2,1)}) %all-gather.21.cloned.1.call-update) | async-done | bytes 8388624 | tf_op jit(solution)/shard_map/all_gather | solution.py:99
  442.3 7.0 fusion.66
  449.3 118.5 %all-gather.23.cloned.1.call-done = bf16[2048,2048]{1,0:T(8,128)(2,1)} async-done(((bf16[256,2048]{1,0:T(8,128)(2,1)}), bf16[2048,2048]{1,0:T(8,128)(2,1)}) %all-gather.23.cloned.1.call-update) | async-done | bytes 8388624 | tf_op jit(solution)/shard_map/all_gather | solution.py:100
  567.8 7.0 fusion.67
  574.8 118.8 %all-gather.25.cloned.1.call-done = bf16[2048,2048]{1,0:T(8,128)(2,1)} async-done(((bf16[2048,256]{1,0:T(8,128)(2,1)}), bf16[2048,2048]{1,0:T(8,128)(2,1)}) %all-gather.25.cloned.1.call-update) | async-done | bytes 8388624 | tf_op jit(solution)/shard_map/all_gather | solution.py:101
  693.6 9.0 multiply_convert_fusion.1
  702.6 6.6 fusion.68
  709.2 3.7 convolution_add_fusion.2
  714.9 7.4 convolution_convert_fusion.7
  722.4 40.2 %all-reduce.14.cloned.1.call-done = f32[256,2048]{1,0:T(8,128)} async-done(((f32[256,2048]{1,0:T(8,128)}), f32[256,2048]{1,0:T(8,128)}) %all-reduce.14.cloned.1.call-update) | async-done | bytes 2097168 | tf_op jit(solution)/shard_map/psum | solution.py:195
  762.6 2.8 multiply_reduce_fusion
  768.8 173.2 %while.40 = (s32[]{:T(128)}, bf16[2,256,512]{1,2,0:T(8,128)(2,1)}, f32[2,256,512]{1,2,0:T(8,128)S(1)}, f32[256,8,64]{0,2,1:T(8,128)}, s32[256]{0:T(256)}, /*inde...) while((s32[]{:T(128)}, bf16[2,256,512]{1,2,0:T(8,128)(2,1)}, ...), condition=%wide.region_14.15_spmd.clone, body=%wide.region_12.14_spmd.clone.sunk | while | flops 340866304 | bytes 25116048 | solution.py:244
  779.5 34.0 %collective-permute-done = bf16[2,256,512]{1,2,0:T(8,128)(2,1)} collective-permute-done((bf16[2,256,512]{1,2,0:T(8,128)(2,1)S(1)}, bf16[2,256,512]{1,2,0:T(8,128)(2,1)}, u32[]{:S(2)}, u32[]{:S(2)}) %collective-permute-start) | collective-permute-done | bytes 524320 | tf_op jit(solution)/shard_map/while/body/eval_jaxpr/ppermute | solution.py:16
  821.2 2.3 fusion.157
  823.4 33.8 %collective-permute-done = bf16[2,256,512]{1,2,0:T(8,128)(2,1)} collective-permute-done((bf16[2,256,512]{1,2,0:T(8,128)(2,1)S(1)}, bf16[2,256,512]{1,2,0:T(8,128)(2,1)}, u32[]{:S(2)}, u32[]{:S(2)}) %collective-permute-start) | collective-permute-done | bytes 524320 | tf_op jit(solution)/shard_map/while/body/eval_jaxpr/ppermute | solution.py:16
  863.8 2.3 fusion.157
  866.0 34.1 %collective-permute-done = bf16[2,256,512]{1,2,0:T(8,128)(2,1)} collective-permute-done((bf16[2,256,512]{1,2,0:T(8,128)(2,1)S(1)}, bf16[2,256,512]{1,2,0:T(8,128)(2,1)}, u32[]{:S(2)}, u32[]{:S(2)}) %collective-permute-start) | collective-permute-done | bytes 524320 | tf_op jit(solution)/shard_map/while/body/eval_jaxpr/ppermute | solution.py:16
  906.6 2.3 fusion.157
  908.9 33.2 %collective-permute-done = bf16[2,256,512]{1,2,0:T(8,128)(2,1)} collective-permute-done((bf16[2,256,512]{1,2,0:T(8,128)(2,1)S(1)}, bf16[2,256,512]{1,2,0:T(8,128)(2,1)}, u32[]{:S(2)}, u32[]{:S(2)}) %collective-permute-start) | collective-permute-done | bytes 524320 | tf_op jit(solution)/shard_map/while/body/eval_jaxpr/ppermute | solution.py:16
  950.8 3.6 convolution_convert_fusion.3
  955.7 2.2 convolution_convert_fusion.6
  957.9 2.3 convolution_convert_fusion.5
  960.5 2.2 convolution_convert_fusion.4
  963.9 5.7 convolution_convert_fusion.2
  970.8 5.7 convolution_convert_fusion.1
  978.1 5.7 convolution_convert_fusion
  985.6 13.9 all-reduce.16.cloned.1.call-done
  999.5 2.3 fusion.27
  1001.8 22.1 %all-reduce.6 = (bf16[2048]{0:T(1024)(128)(2,1)S(1)}, bf16[2048]{0:T(1024)(128)(2,1)S(1)}) all-reduce(bf16[2048]{0:T(1024)(128)(2,1)S(1)} %get-tuple-element.603, bf16[2048]{0:T(1024)(128)(2,1)S(1)} %copy-done.34), channel_id=9, replica_groups=mesh['seq'=2,'ctx'=4,'tp'=4] {'seq','ctx'}, use_global_device_ids=true, to_apply=%region_25.26.clone | all-reduce | flops 4096 | bytes 16384
  1025.2 2.7 add_convert_fusion
  1027.9 1.9 fusion.32
  1029.8 42.1 %reduce-scatter.14.cloned.1.call-done = bf16[512,256]{1,0:T(8,128)(2,1)} async-done(((bf16[512,2048]{1,0:T(8,128)(2,1)}), bf16[512,256]{1,0:T(8,128)(2,1)}) %reduce-scatter.14.cloned.1.call-update) | async-done | bytes 262160 | tf_op jit(solution)/shard_map/reduce_scatter | solution.py:271
  1071.9 1.8 convert_element_type.204
  1073.7 69.6 %reduce-scatter.8.cloned.1.call-done = bf16[256,512]{1,0:T(8,128)(2,1)} async-done(((bf16[2048,512]{1,0:T(8,128)(2,1)}), bf16[256,512]{1,0:T(8,128)(2,1)}) %reduce-scatter.8.cloned.1.call-update) | async-done | bytes 262160 | tf_op jit(solution)/shard_map/reduce_scatter | solution.py:262
  1143.3 1.8 convert_element_type.198
  1145.1 68.9 %reduce-scatter.10.cloned.1.call-done = bf16[256,512]{1,0:T(8,128)(2,1)} async-done(((bf16[2048,512]{1,0:T(8,128)(2,1)}), bf16[256,512]{1,0:T(8,128)(2,1)}) %reduce-scatter.10.cloned.1.call-update) | async-done | bytes 262160 | tf_op jit(solution)/shard_map/reduce_scatter | solution.py:265
  1213.9 1.8 convert_element_type.200
  1215.7 68.9 %reduce-scatter.12.cloned.1.call-done = bf16[256,512]{1,0:T(8,128)(2,1)} async-done(((bf16[2048,512]{1,0:T(8,128)(2,1)}), bf16[256,512]{1,0:T(8,128)(2,1)}) %reduce-scatter.12.cloned.1.call-update) | async-done | bytes 262160 | tf_op jit(solution)/shard_map/reduce_scatter | solution.py:268
  1284.6 1.8 convert_element_type.202
  1286.4 150.1 %reduce-scatter.16.cloned.1.call-done = bf16[256,2048]{1,0:T(8,128)(2,1)} async-done(((bf16[2048,2048]{1,0:T(8,128)(2,1)}), bf16[256,2048]{1,0:T(8,128)(2,1)}) %reduce-scatter.16.cloned.1.call-update) | async-done | bytes 1048592 | tf_op jit(solution)/shard_map/reduce_scatter | solution.py:274
  1436.5 2.8 convert_element_type.206
  1439.3 148.7 %reduce-scatter.18.cloned.1.call-done = bf16[256,2048]{1,0:T(8,128)(2,1)} async-done(((bf16[2048,2048]{1,0:T(8,128)(2,1)}), bf16[256,2048]{1,0:T(8,128)(2,1)}) %reduce-scatter.18.cloned.1.call-update) | async-done | bytes 1048592 | tf_op jit(solution)/shard_map/reduce_scatter | solution.py:277
  1588.0 2.8 convert_element_type.208
  1590.8 149.6 %reduce-scatter.20.cloned.1.call-done = bf16[2048,256]{1,0:T(8,128)(2,1)} async-done(((bf16[2048,2048]{1,0:T(8,128)(2,1)}), bf16[2048,256]{1,0:T(8,128)(2,1)}) %reduce-scatter.20.cloned.1.call-update) | async-done | bytes 1048592 | tf_op jit(solution)/shard_map/reduce_scatter | solution.py:280
  1740.5 2.7 convert_element_type.210
  (264 shorter events, 86.1 us)
Async XLA Ops:
  7.2 27.1 %copy-start.2 = (bf16[256,2048]{1,0:T(8,128)(2,1)S(1)}, bf16[256,2048]{1,0:T(8,128)(2,1)}, u32[]{:S(2)}) copy-start(bf16[256,2048]{1,0:T(8,128)(2,1)} %param.16) | copy-start | bytes 3145732
  7.2 55.0 %all-gather.11.cloned.1.call-start = ((), (), s32[]{:S(2)}) async-start(), calls=%async_computation.7 | async-start | bytes 2359296 | tf_op jit(solution)/shard_map/all_gather | solution.py:96
  7.9 104.2 %all-gather.17.cloned.1.call-start = ((), (), s32[]{:S(2)}) async-start(), calls=%async_computation.10 | async-start | bytes 2359296 | tf_op jit(solution)/shard_map/all_gather | solution.py:95
  8.7 153.4 %all-gather.13.cloned.1.call-start = ((), (), s32[]{:S(2)}) async-start(), calls=%async_computation.8 | async-start | bytes 2359296 | tf_op jit(solution)/shard_map/all_gather | solution.py:97
  9.4 200.5 %all-gather.15.cloned.1.call-start = ((), (), s32[]{:S(2)}) async-start(), calls=%async_computation.9 | async-start | bytes 2621440 | tf_op jit(solution)/shard_map/all_gather | solution.py:132
  34.5 30.0 %copy-start.35 = (f32[256]{0:T(256)}, f32[256]{0:T(256)S(1)}, u32[]{:S(2)}) copy-start(f32[256]{0:T(256)S(1)} %fusion.33) | copy-start | bytes 3076
  34.6 127.5 %copy-start.30 = (f32[256]{0:T(256)}, f32[256]{0:T(256)S(1)}, u32[]{:S(2)}) copy-start(f32[256]{0:T(256)S(1)} %fusion.49) | copy-start | bytes 3076
  123.1 42.9 %copy-start.27 = (bf16[256,512]{1,0:T(8,128)(2,1)S(1)}, bf16[256,512]{1,0:T(8,128)(2,1)}, u32[]{:S(2)}) copy-start(bf16[256,512]{1,0:T(8,128)(2,1)} %get-tuple-element.660) | copy-start | bytes 786436
  165.3 96.2 %all-gather.19.cloned.1.call-start = ((), (), s32[]{:S(2)}) async-start(), calls=%async_computation.11 | async-start | bytes 2359296 | tf_op jit(solution)/shard_map/all_gather | solution.py:98
  165.9 149.0 %all-reduce.12.cloned.1.call-start = ((), (), s32[]{:S(2)}) async-start(), calls=%async_computation.12 | async-start | bytes 4194304 | tf_op jit(solution)/shard_map/psum | solution.py:156
  233.8 31.3 %copy-start.17 = (bf16[256,512]{0,1:T(8,128)(2,1)}, bf16[256,512]{0,1:T(8,128)(2,1)S(1)}, u32[]{:S(2)}) copy-start(bf16[256,512]{0,1:T(8,128)(2,1)S(1)} %fusion.37) | copy-start | bytes 786436
  265.2 2.3 copy-start.40
  265.2 49.7 %copy-start.3 = (bf16[256,2048]{1,0:T(8,128)(2,1)S(1)}, bf16[256,2048]{1,0:T(8,128)(2,1)}, u32[]{:S(2)}) copy-start(bf16[256,2048]{1,0:T(8,128)(2,1)} %param.16) | copy-start | bytes 3145732
  265.2 177.1 %all-gather.21.cloned.1.call-start = ((), (), s32[]{:S(2)}) async-start(), calls=%async_computation.13 | async-start | bytes 9437184 | tf_op jit(solution)/shard_map/all_gather | solution.py:99
  266.0 301.8 %all-gather.23.cloned.1.call-start = ((), (), s32[]{:S(2)}) async-start(), calls=%async_computation.14 | async-start | bytes 9437184 | tf_op jit(solution)/shard_map/all_gather | solution.py:100
  266.7 426.9 %all-gather.25.cloned.1.call-start = ((), (), s32[]{:S(2)}) async-start(), calls=%async_computation.15 | async-start | bytes 9437184 | tf_op jit(solution)/shard_map/all_gather | solution.py:101
  267.5 495.2 %all-reduce.14.cloned.1.call-start = ((), (), s32[]{:S(2)}) async-start(), calls=%async_computation.16 | async-start | bytes 4194304 | tf_op jit(solution)/shard_map/psum | solution.py:195
  314.9 2.6 copy-start.28
  316.9 448.6 %copy-start = (f32[256,2048]{1,0:T(8,128)}, f32[256,2048]{1,0:T(8,128)S(1)}, u32[]{:S(2)}) copy-start(f32[256,2048]{1,0:T(8,128)S(1)} %get-tuple-element.644) | copy-start | bytes 6291460
  317.8 250.0 %copy-start.9 = (bf16[256,2048]{1,0:T(8,128)(2,1)}, bf16[256,2048]{1,0:T(8,128)(2,1)S(1)}, u32[]{:S(2)}) copy-start(bf16[256,2048]{1,0:T(8,128)(2,1)S(1)} %multiply_convert_fusion.3) | copy-start | bytes 3145732
  702.6 6.6 copy-start.25
  702.6 6.6 copy-start.23
  702.6 6.6 copy-start.39
  712.9 1.0 copy-start.13
  712.9 286.6 %all-reduce.16.cloned.1.call-start = ((), (), s32[]{:S(2)}) async-start(), calls=%async_computation.24 | async-start | bytes 4194304 | tf_op jit(solution)/shard_map/psum | solution.py:163
  714.9 47.7 %copy-start.29 = (f32[8,1,256]{2,1,0:T(1,128)S(1)}, f32[8,1,256]{2,1,0:T(1,128)}, u32[]{:S(2)}) copy-start(f32[8,1,256]{2,1,0:T(1,128)} %convert_element_type.216) | copy-start | bytes 24580
  714.9 47.7 %copy-start.33 = (f32[256]{0:T(256)S(1)}, f32[256]{0:T(256)}, u32[]{:S(2)}) copy-start(f32[256]{0:T(256)} %copy-done.32) | copy-start | bytes 3076
  722.4 43.1 %copy-start.38 = (f32[256]{0:T(256)S(1)}, f32[256]{0:T(256)}, u32[]{:S(2)}) copy-start(f32[256]{0:T(256)} %copy-done.37) | copy-start | bytes 3076
  762.6 2.9 copy-start.12
  762.6 2.9 copy-start.14
  765.5 1.0 copy-start.8
  765.5 1.8 copy-start.11
  767.3 1.4 copy-start.5
  775.3 38.2 %collective-permute-start.1 = (f32[2,256,512]{1,2,0:T(8,128)}, f32[2,256,512]{1,2,0:T(8,128)S(1)}, u32[]{:S(2)}, u32[]{:S(2)}) collective-permute-start(f32[2,256,512]{1,2,0:T(8,128)} %maximum_add_fusion.2), channel_id=1, source_target_pairs={{12,0},{0,4},{4,8},{8,12},{13,1},{1,5},{5,9},{9,13},{14,2},{2,6},{... | collective-permute-start | bytes 3145736 | tf_op jit(solution)/shard_map/while/body/eval_jaxpr/ppermute | solution.py:16
  776.8 36.7 %collective-permute-start = (bf16[2,256,512]{1,2,0:T(8,128)(2,1)S(1)}, bf16[2,256,512]{1,2,0:T(8,128)(2,1)}, u32[]{:S(2)}, u32[]{:S(2)}) collective-permute-start(bf16[2,256,512]{1,2,0:T(8,128)(2,1)S(1)} %copy.95), channel_id=1, source_target_pairs={{12,0},{0,4},{4,8},{8,12},{13,1},{1,5},{5,9},{9,13},{14,2},{2,6},{... | collective-permute-start | bytes 1572872 | tf_op jit(solution)/shard_map/while/body/eval_jaxpr/ppermute | solution.py:16
  820.0 37.3 %collective-permute-start.1 = (f32[2,256,512]{1,2,0:T(8,128)}, f32[2,256,512]{1,2,0:T(8,128)S(1)}, u32[]{:S(2)}, u32[]{:S(2)}) collective-permute-start(f32[2,256,512]{1,2,0:T(8,128)} %maximum_add_fusion.2), channel_id=1, source_target_pairs={{12,0},{0,4},{4,8},{8,12},{13,1},{1,5},{5,9},{9,13},{14,2},{2,6},{... | collective-permute-start | bytes 3145736 | tf_op jit(solution)/shard_map/while/body/eval_jaxpr/ppermute | solution.py:16
  820.0 37.3 %collective-permute-start = (bf16[2,256,512]{1,2,0:T(8,128)(2,1)S(1)}, bf16[2,256,512]{1,2,0:T(8,128)(2,1)}, u32[]{:S(2)}, u32[]{:S(2)}) collective-permute-start(bf16[2,256,512]{1,2,0:T(8,128)(2,1)S(1)} %copy.95), channel_id=1, source_target_pairs={{12,0},{0,4},{4,8},{8,12},{13,1},{1,5},{5,9},{9,13},{14,2},{2,6},{... | collective-permute-start | bytes 1572872 | tf_op jit(solution)/shard_map/while/body/eval_jaxpr/ppermute | solution.py:16
  863.8 36.4 %collective-permute-start.1 = (f32[2,256,512]{1,2,0:T(8,128)}, f32[2,256,512]{1,2,0:T(8,128)S(1)}, u32[]{:S(2)}, u32[]{:S(2)}) collective-permute-start(f32[2,256,512]{1,2,0:T(8,128)} %maximum_add_fusion.2), channel_id=1, source_target_pairs={{12,0},{0,4},{4,8},{8,12},{13,1},{1,5},{5,9},{9,13},{14,2},{2,6},{... | collective-permute-start | bytes 3145736 | tf_op jit(solution)/shard_map/while/body/eval_jaxpr/ppermute | solution.py:16
  863.8 36.4 %collective-permute-start = (bf16[2,256,512]{1,2,0:T(8,128)(2,1)S(1)}, bf16[2,256,512]{1,2,0:T(8,128)(2,1)}, u32[]{:S(2)}, u32[]{:S(2)}) collective-permute-start(bf16[2,256,512]{1,2,0:T(8,128)(2,1)S(1)} %copy.95), channel_id=1, source_target_pairs={{12,0},{0,4},{4,8},{8,12},{13,1},{1,5},{5,9},{9,13},{14,2},{2,6},{... | collective-permute-start | bytes 1572872 | tf_op jit(solution)/shard_map/while/body/eval_jaxpr/ppermute | solution.py:16
  906.6 35.5 %collective-permute-start.1 = (f32[2,256,512]{1,2,0:T(8,128)}, f32[2,256,512]{1,2,0:T(8,128)S(1)}, u32[]{:S(2)}, u32[]{:S(2)}) collective-permute-start(f32[2,256,512]{1,2,0:T(8,128)} %maximum_add_fusion.2), channel_id=1, source_target_pairs={{12,0},{0,4},{4,8},{8,12},{13,1},{1,5},{5,9},{9,13},{14,2},{2,6},{... | collective-permute-start | bytes 3145736 | tf_op jit(solution)/shard_map/while/body/eval_jaxpr/ppermute | solution.py:16
  906.6 35.5 %collective-permute-start = (bf16[2,256,512]{1,2,0:T(8,128)(2,1)S(1)}, bf16[2,256,512]{1,2,0:T(8,128)(2,1)}, u32[]{:S(2)}, u32[]{:S(2)}) collective-permute-start(bf16[2,256,512]{1,2,0:T(8,128)(2,1)S(1)} %copy.95), channel_id=1, source_target_pairs={{12,0},{0,4},{4,8},{8,12},{13,1},{1,5},{5,9},{9,13},{14,2},{2,6},{... | collective-permute-start | bytes 1572872 | tf_op jit(solution)/shard_map/while/body/eval_jaxpr/ppermute | solution.py:16
  942.1 1.3 copy-start.7
  943.4 1.6 copy-start.20
  944.9 1.6 copy-start.19
  946.5 1.6 copy-start.21
  949.9 122.0 %reduce-scatter.14.cloned.1.call-start = ((), (), s32[]{:S(2)}) async-start(), calls=%async_computation.20 | async-start | bytes 2359296 | tf_op jit(solution)/shard_map/reduce_scatter | solution.py:271
  954.5 1.2 copy-start.4
  954.5 1.2 copy-start.31
  954.5 188.8 %reduce-scatter.8.cloned.1.call-start = ((), (), s32[]{:S(2)}) async-start(), calls=%async_computation.17 | async-start | bytes 2359296 | tf_op jit(solution)/shard_map/reduce_scatter | solution.py:262
  957.9 256.0 %reduce-scatter.10.cloned.1.call-start = ((), (), s32[]{:S(2)}) async-start(), calls=%async_computation.18 | async-start | bytes 2359296 | tf_op jit(solution)/shard_map/reduce_scatter | solution.py:265
  960.3 2.5 copy-start.10
  960.3 324.3 %reduce-scatter.12.cloned.1.call-start = ((), (), s32[]{:S(2)}) async-start(), calls=%async_computation.19 | async-start | bytes 2359296 | tf_op jit(solution)/shard_map/reduce_scatter | solution.py:268
  962.7 1.2 copy-start.26
  962.7 473.8 %reduce-scatter.16.cloned.1.call-start = ((), (), s32[]{:S(2)}) async-start(), calls=%async_computation.21 | async-start | bytes 9437184 | tf_op jit(solution)/shard_map/reduce_scatter | solution.py:274
  969.6 1.2 copy-start.24
  969.6 618.4 %reduce-scatter.18.cloned.1.call-start = ((), (), s32[]{:S(2)}) async-start(), calls=%async_computation.22 | async-start | bytes 9437184 | tf_op jit(solution)/shard_map/reduce_scatter | solution.py:277
  976.5 1.2 copy-start.15
  976.5 1.5 copy-start.22
  976.5 763.9 %reduce-scatter.20.cloned.1.call-start = ((), (), s32[]{:S(2)}) async-start(), calls=%async_computation.23 | async-start | bytes 9437184 | tf_op jit(solution)/shard_map/reduce_scatter | solution.py:280
  983.8 18.1 %copy-start.34 = (bf16[2048]{0:T(1024)(128)(2,1)S(1)}, bf16[2048]{0:T(1024)(128)(2,1)}, u32[]{:S(2)}) copy-start(bf16[2048]{0:T(1024)(128)(2,1)} %get-tuple-element.601) | copy-start | bytes 12292
  983.8 41.4 %copy-start.36 = (f32[256]{0:T(256)S(1)}, f32[256]{0:T(256)}, u32[]{:S(2)}) copy-start(f32[256]{0:T(256)} %copy-done.35) | copy-start | bytes 3076
  983.8 41.4 %copy-start.1 = (f32[256,2048]{1,0:T(8,128)S(1)}, f32[256,2048]{1,0:T(8,128)}, u32[]{:S(2)}) copy-start(f32[256,2048]{1,0:T(8,128)} %copy-done) | copy-start | bytes 6291460
  1025.2 2.7 copy-start.6
  1025.2 2.7 copy-start.16
  (4 other events, 2.8 us)
Sparse Core Ops, SparseCore 0:
  10.1 52.0 all-gather.10
  64.3 47.7 all-gather.16
  114.3 47.7 all-gather.12
  165.4 44.4 all-gather.14
  211.7 49.7 all-gather.18
  265.3 49.5 all-reduce.11
  317.3 125.0 all-gather.20
  444.7 123.1 all-gather.22
  570.0 123.5 all-gather.24
  713.0 49.5 all-reduce.13
  950.0 49.4 all-reduce.15
  1003.4 68.4 reduce-scatter.13
  1076.4 66.8 reduce-scatter.7
  1147.1 66.8 reduce-scatter.9
  1217.7 66.8 reduce-scatter.11
  1288.5 147.9 reduce-scatter.15
  1440.0 147.9 reduce-scatter.17
  1592.0 148.4 reduce-scatter.19
where the time goes:
time: 1760 us; the launch traced here: 1750 us
  waiting for transfers between devices  1470 us (84%)
  matrix products  106 us (6%)
  other arithmetic  63.6 us (4%)
  blocking collectives  62.5 us (4%)
  local copies, waits for them, and re-layouts  28.8 us (2%)
    reduce_scatter x1, waiting for transfers between devices, per_device(): lax.psum_scatter(gate_wgrad.astype(jnp.bfloat16), ('seq', 'ctx'), scatter...  150 us
    reduce_scatter x1, waiting for transfers between devices, per_device(): lax.psum_scatter(down_grad.astype(jnp.bfloat16), ('seq', 'ctx'), scatter_...  150 us
    reduce_scatter x1, waiting for transfers between devices, per_device(): lax.psum_scatter(upward_wgrad.astype(jnp.bfloat16), ('seq', 'ctx'), scatt...  149 us
    ppermute x8, waiting for transfers between devices, shifted(): return lax.ppermute(block, axis, route)  135 us
    all_gather x1, waiting for transfers between devices, per_device(): lax.all_gather(gate_weight, ('seq', 'ctx'), axis=0, tiled=True)  125 us
    all_gather x1, waiting for transfers between devices, per_device(): lax.all_gather(down_weight, ('seq', 'ctx'), axis=1, tiled=True)  119 us
    all_gather x1, waiting for transfers between devices, per_device(): lax.all_gather(up_weight, ('seq', 'ctx'), axis=0, tiled=True)  118 us
    reduce_scatter x1, waiting for transfers between devices, per_device(): lax.psum_scatter(query_wgrad.astype(jnp.bfloat16), ('seq', 'ctx'), scatte...  69.6 us
  transfers between devices with their start and end apart: 26, of which 22 were waited for; matrix products, arithmetic and copies ran while one was open for 7% of the time, Pallas kernels for 0%

commit v1 on v0

--- a/solution.py
+++ b/solution.py
@@ -1,3 +1,4 @@
+import functools
 from functools import partial
 import jax
 import jax.numpy as jnp
@@ -8,6 +9,24 @@
 BLOCK = 128
 THETA = 130000.0
 EPS = 1e-05
+
+
+def _search_object(u, axis_name, dim_i):
+    outer = lax.psum(1, axis_name)
+    p_next = lax.axis_index(axis_name)
+    mid_arr, tile_out, state_now = (outer, p_next, u.shape[dim_i])
+    by_rank = [kk * mid_arr if dev == dim_i else kk for dev, kk in enumerate(u.shape)]
+    block_next = jnp.zeros(by_rank, u.dtype)
+    later = lax.dynamic_update_slice_in_dim(block_next, u, tile_out * state_now, axis=dim_i)
+    for jj in range(1, mid_arr):
+        u = lax.ppermute(u, axis_name, [(dev, (dev + 1) % mid_arr) for dev in range(mid_arr)])
+        later = lax.dynamic_update_slice_in_dim(
+            later, u, (tile_out - jj) % mid_arr * state_now, axis=dim_i
+        )
+    return later
+
+
+launch_sectors = functools.partial(_search_object, axis_name=("seq", "ctx"), dim_i=0)
 
 
 def shifted(block, axis, distance):
@@ -94,7 +113,7 @@
     gathered = (
         lax.all_gather(query_weight, ("seq", "ctx"), axis=0, tiled=True),
         lax.all_gather(key_weight, ("seq", "ctx"), axis=0, tiled=True),
-        lax.all_gather(value_weight, ("seq", "ctx"), axis=0, tiled=True),
+        launch_sectors(value_weight),
         lax.all_gather(output_weight, ("seq", "ctx"), axis=1, tiled=True),
         lax.all_gather(gate_weight, ("seq", "ctx"), axis=0, tiled=True),
         lax.all_gather(up_weight, ("seq", "ctx"), axis=0, tiled=True),

time: 1760 us -> 1760 us (level)
    ppermute x0 -> x7, waiting for transfers between devices: none -> 70.3 us  [_search_object(): lax.ppermute(u, axis_name, [(dev, (dev + 1) % mid_arr) for dev in range(m...]
    all_gather x1, waiting for transfers between devices: 47.4 us -> 7.93 us  [per_device(): lax.all_gather(query_weight, ('seq', 'ctx'), axis=0, tiled=True)]
    all_gather x1, waiting for transfers between devices: 39 us -> 0.01 us  [per_device(): lax.all_gather(value_weight, ('seq', 'ctx'), axis=0, tiled=True)]
    all_gather x1, waiting for transfers between devices: 27.6 us -> 0.02 us  [per_device(): lax.all_gather(key_weight, ('seq', 'ctx'), axis=0, tiled=True)]
    ppermute x8, waiting for transfers between devices: 135 us -> 162 us  [shifted(): return lax.ppermute(block, axis, route)]
  transfers between devices with their start and end apart: 26 -> 33, of which waited for: 22 -> 26; matrix products, arithmetic and copies ran while one was open for 7% -> 9% of each run, Pallas kernels for 0% -> 0%
where the time goes in v1:
time: 1760 us; the launch traced here: 1750 us
  waiting for transfers between devices  1460 us (83%)
  matrix products  108 us (6%)
  blocking collectives  63.8 us (4%)
  other arithmetic  61.1 us (3%)
  local copies, waits for them, and re-layouts  30.3 us (2%)
    ppermute x8, waiting for transfers between devices, shifted(): return lax.ppermute(block, axis, route)  162 us
    reduce_scatter x1, waiting for transfers between devices, per_device(): lax.psum_scatter(upward_wgrad.astype(jnp.bfloat16), ('seq', 'ctx'), scatt...  150 us
    reduce_scatter x1, waiting for transfers between devices, per_device(): lax.psum_scatter(down_grad.astype(jnp.bfloat16), ('seq', 'ctx'), scatter_...  150 us
    reduce_scatter x1, waiting for transfers between devices, per_device(): lax.psum_scatter(gate_wgrad.astype(jnp.bfloat16), ('seq', 'ctx'), scatter...  149 us
    all_gather x1, waiting for transfers between devices, per_device(): lax.all_gather(gate_weight, ('seq', 'ctx'), axis=0, tiled=True)  124 us
    all_gather x1, waiting for transfers between devices, per_device(): lax.all_gather(down_weight, ('seq', 'ctx'), axis=1, tiled=True)  119 us
    all_gather x1, waiting for transfers between devices, per_device(): lax.all_gather(up_weight, ('seq', 'ctx'), axis=0, tiled=True)  118 us
    ppermute x7, waiting for transfers between devices, _search_object(): lax.ppermute(u, axis_name, [(dev, (dev + 1) % mid_arr) for dev in range(m...  70.3 us
  transfers between devices with their start and end apart: 33, of which 26 were waited for; matrix products, arithmetic and copies ran while one was open for 9% of the time, Pallas kernels for 0%

profile of v1, /device:TPU:0, one launch (start us, length us, event | category | flops | bytes accessed | tf_op | source)
XLA Modules:
  0.0 1748.1 jit_solution(11240490849333565688)
XLA Ops:
  8.7 3.1 collective-permute-start.2
  12.0 9.4 collective-permute-done.2
  22.3 15.9 collective-permute-done.3
  39.5 7.9 collective-permute-done.4
  47.5 16.1 collective-permute-done.5
  63.8 23.6 %all-gather = bf16[8,1,256]{2,1,0:T(2,128)(2,1)S(1)} all-gather(bf16[1,1,256]{2,1,0:T(2,128)(2,1)S(1)} %reshape.359), channel_id=1, replica_groups=mesh['seq'=2,'ctx'=4,'tp'=4] {'seq','ctx'}, dimensions={0}, use_global_device_ids=true | all-gather | bytes 4608 | tf_op jit(solution)/shard_map/all_gather | solution.py:121
  88.3 2.0 copy.60
  94.5 9.5 collective-permute-done.7
  106.0 11.6 collective-permute-done.8
  118.4 2.3 fusion.57
  121.0 7.9 all-gather.15.cloned.1.call-done
  128.9 2.3 fusion.54
  134.6 45.1 %all-gather.13.cloned.1.call-done = bf16[2,1024,512]{2,1,0:T(8,128)(2,1)} async-done(((bf16[2,256,512]{2,1,0:T(8,128)(2,1)}), bf16[2,1024,512]{2,1,0:T(8,128)(2,1)}) %all-gather.13.cloned.1.call-update) | async-done | bytes 2097168 | tf_op jit(solution)/shard_map/all_gather | solution.py:151
  179.7 22.9 %while.39 = (s32[]{:T(128)}, f32[256,8]{0,1:T(8,128)S(1)}, f32[256,512]{0,1:T(8,128)}, s32[256]{0:T(256)}, s32[8]{0:T(128)}, /*index=5*/bf16[2,1024,512]{2,1,0:T...) while((s32[]{:T(128)}, f32[256,8]{0,1:T(8,128)S(1)}, ...), condition=%wide.region_5.6_spmd.clone, body=%wide.region_2.5_spmd.clone.sunk | while | flops 137706752 | bytes 9411818 | solution.py:170
  188.7 1.9 bitcast_add_fusion.5
  194.7 1.9 bitcast_add_fusion.5
  203.6 27.7 %all-gather.17.cloned.1.call-done = bf16[512,2048]{1,0:T(8,128)(2,1)} async-done(((bf16[512,256]{1,0:T(8,128)(2,1)}), bf16[512,2048]{1,0:T(8,128)(2,1)}) %all-gather.17.cloned.1.call-update) | async-done | bytes 2097168 | tf_op jit(solution)/shard_map/all_gather | solution.py:117
  231.4 3.6 fusion.65
  237.2 18.2 %all-gather.1 = bf16[8,1,256]{2,1,0:T(2,128)(2,1)S(1)} all-gather(bf16[1,1,256]{2,1,0:T(2,128)(2,1)S(1)} %reshape.361), channel_id=1, replica_groups=mesh['seq'=2,'ctx'=4,'tp'=4] {'seq','ctx'}, dimensions={0}, use_global_device_ids=true | all-gather | bytes 4608 | tf_op jit(solution)/shard_map/all_gather | solution.py:122
  256.0 28.8 %all-reduce.12.cloned.1.call-done = f32[256,2048]{1,0:T(8,128)} async-done(((f32[256,2048]{1,0:T(8,128)}), f32[256,2048]{1,0:T(8,128)}) %all-reduce.12.cloned.1.call-update) | async-done | bytes 2097168 | tf_op jit(solution)/shard_map/psum | solution.py:175
  284.8 2.0 multiply_reduce_fusion.2
  287.6 124.4 %all-gather.19.cloned.1.call-done = bf16[2048,2048]{1,0:T(8,128)(2,1)} async-done(((bf16[256,2048]{1,0:T(8,128)(2,1)}), bf16[2048,2048]{1,0:T(8,128)(2,1)}) %all-gather.19.cloned.1.call-update) | async-done | bytes 8388624 | tf_op jit(solution)/shard_map/all_gather | solution.py:118
  412.0 7.0 fusion.66
  419.0 118.5 %all-gather.21.cloned.1.call-done = bf16[2048,2048]{1,0:T(8,128)(2,1)} async-done(((bf16[256,2048]{1,0:T(8,128)(2,1)}), bf16[2048,2048]{1,0:T(8,128)(2,1)}) %all-gather.21.cloned.1.call-update) | async-done | bytes 8388624 | tf_op jit(solution)/shard_map/all_gather | solution.py:119
  537.5 7.0 fusion.67
  544.5 118.8 %all-gather.23.cloned.1.call-done = bf16[2048,2048]{1,0:T(8,128)(2,1)} async-done(((bf16[2048,256]{1,0:T(8,128)(2,1)}), bf16[2048,2048]{1,0:T(8,128)(2,1)}) %all-gather.23.cloned.1.call-update) | async-done | bytes 8388624 | tf_op jit(solution)/shard_map/all_gather | solution.py:120
  663.3 9.0 multiply_convert_fusion.1
  672.3 6.5 fusion.68
  678.8 3.7 convolution_add_fusion.2
  684.6 7.4 convolution_convert_fusion.7
  692.1 40.3 %all-reduce.14.cloned.1.call-done = f32[256,2048]{1,0:T(8,128)} async-done(((f32[256,2048]{1,0:T(8,128)}), f32[256,2048]{1,0:T(8,128)}) %all-reduce.14.cloned.1.call-update) | async-done | bytes 2097168 | tf_op jit(solution)/shard_map/psum | solution.py:214
  732.3 2.8 multiply_reduce_fusion
  738.5 199.0 %while.40 = (s32[]{:T(128)}, bf16[2,256,512]{1,2,0:T(8,128)(2,1)}, f32[2,256,512]{1,2,0:T(8,128)S(1)}, f32[256,8,64]{0,2,1:T(8,128)}, s32[256]{0:T(256)}, /*inde...) while((s32[]{:T(128)}, bf16[2,256,512]{1,2,0:T(8,128)(2,1)}, ...), condition=%wide.region_14.15_spmd.clone, body=%wide.region_12.14_spmd.clone.sunk | while | flops 340866304 | bytes 25116048 | solution.py:263
  749.2 56.9 %collective-permute-done = bf16[2,256,512]{1,2,0:T(8,128)(2,1)} collective-permute-done((bf16[2,256,512]{1,2,0:T(8,128)(2,1)S(1)}, bf16[2,256,512]{1,2,0:T(8,128)(2,1)}, u32[]{:S(2)}, u32[]{:S(2)}) %collective-permute-start) | collective-permute-done | bytes 524320 | tf_op jit(solution)/shard_map/while/body/eval_jaxpr/ppermute | solution.py:35
  813.1 2.3 fusion.157
  815.4 35.4 %collective-permute-done = bf16[2,256,512]{1,2,0:T(8,128)(2,1)} collective-permute-done((bf16[2,256,512]{1,2,0:T(8,128)(2,1)S(1)}, bf16[2,256,512]{1,2,0:T(8,128)(2,1)}, u32[]{:S(2)}, u32[]{:S(2)}) %collective-permute-start) | collective-permute-done | bytes 524320 | tf_op jit(solution)/shard_map/while/body/eval_jaxpr/ppermute | solution.py:35
  857.3 2.3 fusion.157
  859.6 35.0 %collective-permute-done = bf16[2,256,512]{1,2,0:T(8,128)(2,1)} collective-permute-done((bf16[2,256,512]{1,2,0:T(8,128)(2,1)S(1)}, bf16[2,256,512]{1,2,0:T(8,128)(2,1)}, u32[]{:S(2)}, u32[]{:S(2)}) %collective-permute-start) | collective-permute-done | bytes 524320 | tf_op jit(solution)/shard_map/while/body/eval_jaxpr/ppermute | solution.py:35
  901.1 2.3 fusion.157
  903.4 34.1 %collective-permute-done = bf16[2,256,512]{1,2,0:T(8,128)(2,1)} collective-permute-done((bf16[2,256,512]{1,2,0:T(8,128)(2,1)S(1)}, bf16[2,256,512]{1,2,0:T(8,128)(2,1)}, u32[]{:S(2)}, u32[]{:S(2)}) %collective-permute-start) | collective-permute-done | bytes 524320 | tf_op jit(solution)/shard_map/while/body/eval_jaxpr/ppermute | solution.py:35
  942.0 2.1 convolution_add_fusion.1
  944.1 4.0 fusion.23
  949.0 3.6 convolution_convert_fusion.3
  953.9 2.2 convolution_convert_fusion.6
  956.1 2.3 convolution_convert_fusion.5
  958.7 2.2 convolution_convert_fusion.4
  962.1 5.7 convolution_convert_fusion.1
  969.0 5.7 convolution_convert_fusion.2
  976.3 5.7 convolution_convert_fusion
  983.9 13.8 all-reduce.16.cloned.1.call-done
  997.7 2.3 fusion.27
  1000.0 22.1 %all-reduce.6 = (bf16[2048]{0:T(1024)(128)(2,1)S(1)}, bf16[2048]{0:T(1024)(128)(2,1)S(1)}) all-reduce(bf16[2048]{0:T(1024)(128)(2,1)S(1)} %get-tuple-element.603, bf16[2048]{0:T(1024)(128)(2,1)S(1)} %copy-done.35), channel_id=9, replica_groups=mesh['seq'=2,'ctx'=4,'tp'=4] {'seq','ctx'}, use_global_device_ids=true, to_apply=%region_25.26.clone | all-reduce | flops 4096 | bytes 16384
  1023.4 2.7 add_convert_fusion
  1026.0 1.9 fusion.32
  1028.0 42.1 %reduce-scatter.14.cloned.1.call-done = bf16[512,256]{1,0:T(8,128)(2,1)} async-done(((bf16[512,2048]{1,0:T(8,128)(2,1)}), bf16[512,256]{1,0:T(8,128)(2,1)}) %reduce-scatter.14.cloned.1.call-update) | async-done | bytes 262160 | tf_op jit(solution)/shard_map/reduce_scatter | solution.py:290
  1071.8 69.6 %reduce-scatter.8.cloned.1.call-done = bf16[256,512]{1,0:T(8,128)(2,1)} async-done(((bf16[2048,512]{1,0:T(8,128)(2,1)}), bf16[256,512]{1,0:T(8,128)(2,1)}) %reduce-scatter.8.cloned.1.call-update) | async-done | bytes 262160 | tf_op jit(solution)/shard_map/reduce_scatter | solution.py:281
  1143.2 68.8 %reduce-scatter.10.cloned.1.call-done = bf16[256,512]{1,0:T(8,128)(2,1)} async-done(((bf16[2048,512]{1,0:T(8,128)(2,1)}), bf16[256,512]{1,0:T(8,128)(2,1)}) %reduce-scatter.10.cloned.1.call-update) | async-done | bytes 262160 | tf_op jit(solution)/shard_map/reduce_scatter | solution.py:284
  1213.8 68.7 %reduce-scatter.12.cloned.1.call-done = bf16[256,512]{1,0:T(8,128)(2,1)} async-done(((bf16[2048,512]{1,0:T(8,128)(2,1)}), bf16[256,512]{1,0:T(8,128)(2,1)}) %reduce-scatter.12.cloned.1.call-update) | async-done | bytes 262160 | tf_op jit(solution)/shard_map/reduce_scatter | solution.py:287
  1284.3 150.1 %reduce-scatter.18.cloned.1.call-done = bf16[256,2048]{1,0:T(8,128)(2,1)} async-done(((bf16[2048,2048]{1,0:T(8,128)(2,1)}), bf16[256,2048]{1,0:T(8,128)(2,1)}) %reduce-scatter.18.cloned.1.call-update) | async-done | bytes 1048592 | tf_op jit(solution)/shard_map/reduce_scatter | solution.py:296
  1434.4 2.8 convert_element_type.208
  1437.2 148.8 %reduce-scatter.16.cloned.1.call-done = bf16[256,2048]{1,0:T(8,128)(2,1)} async-done(((bf16[2048,2048]{1,0:T(8,128)(2,1)}), bf16[256,2048]{1,0:T(8,128)(2,1)}) %reduce-scatter.16.cloned.1.call-update) | async-done | bytes 1048592 | tf_op jit(solution)/shard_map/reduce_scatter | solution.py:293
  1586.0 2.8 convert_element_type.206
  1588.8 149.6 %reduce-scatter.20.cloned.1.call-done = bf16[2048,256]{1,0:T(8,128)(2,1)} async-done(((bf16[2048,2048]{1,0:T(8,128)(2,1)}), bf16[2048,256]{1,0:T(8,128)(2,1)}) %reduce-scatter.20.cloned.1.call-update) | async-done | bytes 1048592 | tf_op jit(solution)/shard_map/reduce_scatter | solution.py:299
  1738.3 2.7 convert_element_type.210
  (289 shorter events, 95.2 us)
Async XLA Ops:
  7.2 4.8 copy-start.27
  7.2 14.2 copy-start.2
  7.2 111.2 %all-gather.11.cloned.1.call-start = ((), (), s32[]{:S(2)}) async-start(), calls=%async_computation.7 | async-start | bytes 2359296 | tf_op jit(solution)/shard_map/all_gather | solution.py:115
  7.9 121.0 %all-gather.15.cloned.1.call-start = ((), (), s32[]{:S(2)}) async-start(), calls=%async_computation.9 | async-start | bytes 2359296 | tf_op jit(solution)/shard_map/all_gather | solution.py:114
  8.7 55.1 %copy-start.40 = (bf16[256]{0:T(256)(128)(2,1)S(1)}, bf16[256]{0:T(256)(128)(2,1)}, u32[]{:S(2)}) copy-start(bf16[256]{0:T(256)(128)(2,1)} %param.24) | copy-start | bytes 1540
  8.7 171.0 %all-gather.13.cloned.1.call-start = ((), (), s32[]{:S(2)}) async-start(), calls=%async_computation.8 | async-start | bytes 2621440 | tf_op jit(solution)/shard_map/all_gather | solution.py:151
  8.7 12.7 collective-permute-start.2
  21.4 16.8 collective-permute-start.3
  38.2 9.2 collective-permute-start.4
  47.4 16.2 copy-start.28
  47.4 16.2 collective-permute-start.5
  63.5 27.4 %collective-permute-start.6 = (bf16[256,512]{1,0:T(8,128)(2,1)}, bf16[256,512]{1,0:T(8,128)(2,1)}, u32[]{:S(2)}, u32[]{:S(2)}) collective-permute-start(bf16[256,512]{1,0:T(8,128)(2,1)} %collective-permute-done.5), channel_id=1, source_target_pairs={{0,4},{4,8},{8,12},{12,16},{16,20},{20,24},{24,28},{28,0},{1,5},{5... | collective-permute-start | bytes 786440 | tf_op jit(solution)/shard_map/ppermute | solution.py:22
  91.0 37.9 %copy-start.31 = (f32[256]{0:T(256)}, f32[256]{0:T(256)S(1)}, u32[]{:S(2)}) copy-start(f32[256]{0:T(256)S(1)} %fusion.49) | copy-start | bytes 3076
  91.0 13.0 collective-permute-start.7
  104.0 13.6 collective-permute-start.8
  133.8 97.6 %all-gather.17.cloned.1.call-start = ((), (), s32[]{:S(2)}) async-start(), calls=%async_computation.10 | async-start | bytes 2359296 | tf_op jit(solution)/shard_map/all_gather | solution.py:117
  134.4 150.4 %all-reduce.12.cloned.1.call-start = ((), (), s32[]{:S(2)}) async-start(), calls=%async_computation.11 | async-start | bytes 4194304 | tf_op jit(solution)/shard_map/psum | solution.py:175
  203.6 31.4 %copy-start.17 = (bf16[256,512]{0,1:T(8,128)(2,1)}, bf16[256,512]{0,1:T(8,128)(2,1)S(1)}, u32[]{:S(2)}) copy-start(bf16[256,512]{0,1:T(8,128)(2,1)S(1)} %fusion.37) | copy-start | bytes 786436
  235.0 2.2 copy-start.41
  235.0 49.7 %copy-start.3 = (bf16[256,2048]{1,0:T(8,128)(2,1)S(1)}, bf16[256,2048]{1,0:T(8,128)(2,1)}, u32[]{:S(2)}) copy-start(bf16[256,2048]{1,0:T(8,128)(2,1)} %param.16) | copy-start | bytes 3145732
  235.1 177.0 %all-gather.19.cloned.1.call-start = ((), (), s32[]{:S(2)}) async-start(), calls=%async_computation.12 | async-start | bytes 9437184 | tf_op jit(solution)/shard_map/all_gather | solution.py:118
  235.6 301.9 %all-gather.21.cloned.1.call-start = ((), (), s32[]{:S(2)}) async-start(), calls=%async_computation.13 | async-start | bytes 9437184 | tf_op jit(solution)/shard_map/all_gather | solution.py:119
  236.4 426.9 %all-gather.23.cloned.1.call-start = ((), (), s32[]{:S(2)}) async-start(), calls=%async_computation.14 | async-start | bytes 9437184 | tf_op jit(solution)/shard_map/all_gather | solution.py:120
  237.1 495.2 %all-reduce.14.cloned.1.call-start = ((), (), s32[]{:S(2)}) async-start(), calls=%async_computation.15 | async-start | bytes 4194304 | tf_op jit(solution)/shard_map/psum | solution.py:214
  284.8 2.6 copy-start.29
  286.7 448.5 %copy-start = (f32[256,2048]{1,0:T(8,128)}, f32[256,2048]{1,0:T(8,128)S(1)}, u32[]{:S(2)}) copy-start(f32[256,2048]{1,0:T(8,128)S(1)} %get-tuple-element.644) | copy-start | bytes 6291460
  287.6 249.9 %copy-start.9 = (bf16[256,2048]{1,0:T(8,128)(2,1)}, bf16[256,2048]{1,0:T(8,128)(2,1)S(1)}, u32[]{:S(2)}) copy-start(bf16[256,2048]{1,0:T(8,128)(2,1)S(1)} %multiply_convert_fusion.3) | copy-start | bytes 3145732
  672.3 6.6 copy-start.23
  672.3 6.6 copy-start.25
  672.3 6.6 copy-start.39
  682.6 261.5 %all-gather.25.cloned.1.call-start = ((), (), s32[]{:S(2)}) async-start(), calls=%async_computation.16 | async-start | bytes 2359296 | tf_op jit(solution)/shard_map/all_gather | solution.py:188
  683.2 314.5 %all-reduce.16.cloned.1.call-start = ((), (), s32[]{:S(2)}) async-start(), calls=%async_computation.24 | async-start | bytes 4194304 | tf_op jit(solution)/shard_map/psum | solution.py:182
  684.6 47.7 %copy-start.30 = (f32[8,1,256]{2,1,0:T(1,128)S(1)}, f32[8,1,256]{2,1,0:T(1,128)}, u32[]{:S(2)}) copy-start(f32[8,1,256]{2,1,0:T(1,128)} %convert_element_type.216) | copy-start | bytes 24580
  684.6 47.7 %copy-start.34 = (f32[256]{0:T(256)S(1)}, f32[256]{0:T(256)}, u32[]{:S(2)}) copy-start(f32[256]{0:T(256)} %copy-done.33) | copy-start | bytes 3076
  692.0 43.1 %copy-start.38 = (f32[256]{0:T(256)S(1)}, f32[256]{0:T(256)}, u32[]{:S(2)}) copy-start(f32[256]{0:T(256)} %copy-done.37) | copy-start | bytes 3076
  732.3 2.9 copy-start.12
  732.3 2.9 copy-start.14
  735.2 1.8 copy-start.11
  737.0 1.4 copy-start.5
  745.0 61.1 %collective-permute-start.1 = (f32[2,256,512]{1,2,0:T(8,128)}, f32[2,256,512]{1,2,0:T(8,128)S(1)}, u32[]{:S(2)}, u32[]{:S(2)}) collective-permute-start(f32[2,256,512]{1,2,0:T(8,128)} %maximum_add_fusion.2), channel_id=1, source_target_pairs={{12,0},{0,4},{4,8},{8,12},{13,1},{1,5},{5,9},{9,13},{14,2},{2,6},{... | collective-permute-start | bytes 3145736 | tf_op jit(solution)/shard_map/while/body/eval_jaxpr/ppermute | solution.py:35
  746.5 59.7 %collective-permute-start = (bf16[2,256,512]{1,2,0:T(8,128)(2,1)S(1)}, bf16[2,256,512]{1,2,0:T(8,128)(2,1)}, u32[]{:S(2)}, u32[]{:S(2)}) collective-permute-start(bf16[2,256,512]{1,2,0:T(8,128)(2,1)S(1)} %copy.103), channel_id=1, source_target_pairs={{12,0},{0,4},{4,8},{8,12},{13,1},{1,5},{5,9},{9,13},{14,2},{2,6},{... | collective-permute-start | bytes 1572872 | tf_op jit(solution)/shard_map/while/body/eval_jaxpr/ppermute | solution.py:35
  812.6 38.2 %collective-permute-start.1 = (f32[2,256,512]{1,2,0:T(8,128)}, f32[2,256,512]{1,2,0:T(8,128)S(1)}, u32[]{:S(2)}, u32[]{:S(2)}) collective-permute-start(f32[2,256,512]{1,2,0:T(8,128)} %maximum_add_fusion.2), channel_id=1, source_target_pairs={{12,0},{0,4},{4,8},{8,12},{13,1},{1,5},{5,9},{9,13},{14,2},{2,6},{... | collective-permute-start | bytes 3145736 | tf_op jit(solution)/shard_map/while/body/eval_jaxpr/ppermute | solution.py:35
  812.6 38.2 %collective-permute-start = (bf16[2,256,512]{1,2,0:T(8,128)(2,1)S(1)}, bf16[2,256,512]{1,2,0:T(8,128)(2,1)}, u32[]{:S(2)}, u32[]{:S(2)}) collective-permute-start(bf16[2,256,512]{1,2,0:T(8,128)(2,1)S(1)} %copy.103), channel_id=1, source_target_pairs={{12,0},{0,4},{4,8},{8,12},{13,1},{1,5},{5,9},{9,13},{14,2},{2,6},{... | collective-permute-start | bytes 1572872 | tf_op jit(solution)/shard_map/while/body/eval_jaxpr/ppermute | solution.py:35
  857.3 37.3 %collective-permute-start.1 = (f32[2,256,512]{1,2,0:T(8,128)}, f32[2,256,512]{1,2,0:T(8,128)S(1)}, u32[]{:S(2)}, u32[]{:S(2)}) collective-permute-start(f32[2,256,512]{1,2,0:T(8,128)} %maximum_add_fusion.2), channel_id=1, source_target_pairs={{12,0},{0,4},{4,8},{8,12},{13,1},{1,5},{5,9},{9,13},{14,2},{2,6},{... | collective-permute-start | bytes 3145736 | tf_op jit(solution)/shard_map/while/body/eval_jaxpr/ppermute | solution.py:35
  857.3 37.3 %collective-permute-start = (bf16[2,256,512]{1,2,0:T(8,128)(2,1)S(1)}, bf16[2,256,512]{1,2,0:T(8,128)(2,1)}, u32[]{:S(2)}, u32[]{:S(2)}) collective-permute-start(bf16[2,256,512]{1,2,0:T(8,128)(2,1)S(1)} %copy.103), channel_id=1, source_target_pairs={{12,0},{0,4},{4,8},{8,12},{13,1},{1,5},{5,9},{9,13},{14,2},{2,6},{... | collective-permute-start | bytes 1572872 | tf_op jit(solution)/shard_map/while/body/eval_jaxpr/ppermute | solution.py:35
  901.1 36.4 %collective-permute-start.1 = (f32[2,256,512]{1,2,0:T(8,128)}, f32[2,256,512]{1,2,0:T(8,128)S(1)}, u32[]{:S(2)}, u32[]{:S(2)}) collective-permute-start(f32[2,256,512]{1,2,0:T(8,128)} %maximum_add_fusion.2), channel_id=1, source_target_pairs={{12,0},{0,4},{4,8},{8,12},{13,1},{1,5},{5,9},{9,13},{14,2},{2,6},{... | collective-permute-start | bytes 3145736 | tf_op jit(solution)/shard_map/while/body/eval_jaxpr/ppermute | solution.py:35
  901.1 36.4 %collective-permute-start = (bf16[2,256,512]{1,2,0:T(8,128)(2,1)S(1)}, bf16[2,256,512]{1,2,0:T(8,128)(2,1)}, u32[]{:S(2)}, u32[]{:S(2)}) collective-permute-start(bf16[2,256,512]{1,2,0:T(8,128)(2,1)S(1)} %copy.103), channel_id=1, source_target_pairs={{12,0},{0,4},{4,8},{8,12},{13,1},{1,5},{5,9},{9,13},{14,2},{2,6},{... | collective-permute-start | bytes 1572872 | tf_op jit(solution)/shard_map/while/body/eval_jaxpr/ppermute | solution.py:35
  937.6 1.3 copy-start.7
  938.8 1.6 copy-start.20
  940.4 1.6 copy-start.19
  948.1 122.0 %reduce-scatter.14.cloned.1.call-start = ((), (), s32[]{:S(2)}) async-start(), calls=%async_computation.20 | async-start | bytes 2359296 | tf_op jit(solution)/shard_map/reduce_scatter | solution.py:290
  952.7 188.8 %reduce-scatter.8.cloned.1.call-start = ((), (), s32[]{:S(2)}) async-start(), calls=%async_computation.17 | async-start | bytes 2359296 | tf_op jit(solution)/shard_map/reduce_scatter | solution.py:281
  956.1 255.9 %reduce-scatter.10.cloned.1.call-start = ((), (), s32[]{:S(2)}) async-start(), calls=%async_computation.18 | async-start | bytes 2359296 | tf_op jit(solution)/shard_map/reduce_scatter | solution.py:284
  958.4 2.5 copy-start.10
  958.4 324.0 %reduce-scatter.12.cloned.1.call-start = ((), (), s32[]{:S(2)}) async-start(), calls=%async_computation.19 | async-start | bytes 2359296 | tf_op jit(solution)/shard_map/reduce_scatter | solution.py:287
  960.9 473.5 %reduce-scatter.18.cloned.1.call-start = ((), (), s32[]{:S(2)}) async-start(), calls=%async_computation.22 | async-start | bytes 9437184 | tf_op jit(solution)/shard_map/reduce_scatter | solution.py:296
  967.8 618.1 %reduce-scatter.16.cloned.1.call-start = ((), (), s32[]{:S(2)}) async-start(), calls=%async_computation.21 | async-start | bytes 9437184 | tf_op jit(solution)/shard_map/reduce_scatter | solution.py:293
  974.7 1.5 copy-start.22
  974.8 763.5 %reduce-scatter.20.cloned.1.call-start = ((), (), s32[]{:S(2)}) async-start(), calls=%async_computation.23 | async-start | bytes 9437184 | tf_op jit(solution)/shard_map/reduce_scatter | solution.py:299
  982.0 18.0 %copy-start.35 = (bf16[2048]{0:T(1024)(128)(2,1)S(1)}, bf16[2048]{0:T(1024)(128)(2,1)}, u32[]{:S(2)}) copy-start(bf16[2048]{0:T(1024)(128)(2,1)} %get-tuple-element.601) | copy-start | bytes 12292
  982.0 41.3 %copy-start.36 = (f32[256]{0:T(256)S(1)}, f32[256]{0:T(256)}, u32[]{:S(2)}) copy-start(f32[256]{0:T(256)} %fusion.33) | copy-start | bytes 3076
  982.0 41.3 %copy-start.1 = (f32[256,2048]{1,0:T(8,128)S(1)}, f32[256,2048]{1,0:T(8,128)}, u32[]{:S(2)}) copy-start(f32[256,2048]{1,0:T(8,128)} %copy-done) | copy-start | bytes 6291460
  1023.3 2.7 copy-start.6
  1023.4 2.7 copy-start.16
  (12 other events, 12.1 us)
Sparse Core Ops, SparseCore 0:
  10.2 63.7 all-gather.10
  76.1 52.8 all-gather.14
  133.9 45.7 all-gather.12
  181.5 49.7 all-gather.16
  235.1 49.5 all-reduce.11
  286.9 125.0 all-gather.18
  414.3 123.1 all-gather.20
  539.7 123.5 all-gather.22
  682.7 49.5 all-reduce.13
  734.3 70.0 all-gather.24
  948.2 49.4 all-reduce.15
  1001.5 68.4 reduce-scatter.13
  1074.6 66.8 reduce-scatter.7
  1145.2 66.7 reduce-scatter.9
  1215.8 66.6 reduce-scatter.11
  1286.4 147.9 reduce-scatter.17
  1437.9 148.0 reduce-scatter.15
  1589.9 148.3 reduce-scatter.19
